TPU v7x, 256 devices: a whole 4x4x8 slice. The times are simulated.
256 devices in a mesh: ctx: 64 (over y, z, core), head: 4 (over x).
Axes of the slice: x: 4, y: 4, z: 8, core: 2. Of those that a mesh axis runs over, the one named last changes fastest.
Arguments:
- query: bfloat16 [64, 2, 512, 4096], P('ctx', None, None, 'head'), may hold values from -48 to 48
- key: bfloat16 [64, 2, 512, 512], P('ctx', None, 'head'), may hold values from -18 to 18
- value: bfloat16 [64, 2, 512, 512], P('ctx', None, 'head'), may hold values from -6 to 6
- d_out: bfloat16 [64, 2, 512, 4096], P('ctx', None, None, 'head'), may hold values from -6 to 6
- doc_start: int32 [512], replicated, may hold values from 0 to 1, as said below
Outputs:
- d_query: bfloat16 [64, 2, 512, 4096], P('ctx', None, None, 'head')
- d_key: bfloat16 [64, 2, 512, 512], P('ctx', None, 'head')
- d_value: bfloat16 [64, 2, 512, 512], P('ctx', None, 'head')
Inputs may be any that keep to these rules, and one draw needn't show every extreme that they name: `doc_start`: 1 where a document begins at that block of 128 tokens (blocks in sequence order); block 0 begins one; from every beginning the next beginning, or the end of the sequence, is 1 to 3 blocks away; the first block of every span after the first lies inside a document of exactly 3 blocks that began in the span before.
All inputs are finite; a program needn't handle non-finite values.
Results may differ from a plain program's by a relative error of at most 0.039.
Values may be sent and summed in bfloat16 or wider, within the bound.
A program may use at most 64 MiB of HBM per device.

v0:
```python
import jax
import jax.numpy as jnp
from jax import lax
from jax.sharding import PartitionSpec as P

HD = 128
BLK = 128
GROUP = 8


def padded_2(cells, sides, width):
    for axis, dim in sides:
        count = lax.axis_size(axis)
        ends = count - 1
        head = lax.slice_in_dim(cells, 0, width, axis=dim)
        tail = lax.slice_in_dim(cells, cells.shape[dim] - width, cells.shape[dim], axis=dim)
        cells = jnp.concatenate(
            [
                lax.ppermute(tail, axis, [(i, (i + 1) % count) for i in range(ends)]),
                cells,
                lax.ppermute(head, axis, [((i + 1) % count, i) for i in range(ends)]),
            ],
            axis=dim,
        )
    return cells


def windowed(extended, reach_rows, blocks):
    pieces = []
    for offset in range(reach_rows // BLK + 1):
        sliced = lax.slice_in_dim(extended, offset * BLK, offset * BLK + blocks * BLK, axis=0)
        pieces.append(sliced.reshape((blocks, BLK) + extended.shape[1:]))
    return jnp.concatenate(pieces, axis=1)


def unwindowed(windows, reach_rows, blocks):
    summed = None
    for offset in range(reach_rows // BLK + 1):
        sliced = windows[:, offset * BLK : (offset + 1) * BLK].reshape(
            (blocks * BLK,) + windows.shape[2:]
        )
        padded = jnp.pad(
            sliced, ((offset * BLK, reach_rows - offset * BLK),) + ((0, 0),) * (windows.ndim - 2)
        )
        summed = padded if summed is None else summed + padded
    return summed


def span_grads(queries, grads_out, keys_ext, values_ext, doc_begins, span_start, reach_rows):
    blocks = queries.shape[0] // BLK
    kv_heads = keys_ext.shape[1] // HD
    score_scale = HD ** (-0.5)
    q_blocks = queries.reshape(blocks, BLK, kv_heads, GROUP, HD)
    do_blocks = grads_out.reshape(blocks, BLK, kv_heads, GROUP, HD)
    k_windows = windowed(keys_ext.reshape(-1, kv_heads, HD), reach_rows, blocks)
    v_windows = windowed(values_ext.reshape(-1, kv_heads, HD), reach_rows, blocks)
    row_pos = jnp.arange(BLK, dtype=jnp.int32)[None, :, None]
    col_pos = jnp.arange(reach_rows + BLK, dtype=jnp.int32)[None, None, :]
    key_pos = (
        span_start - reach_rows + jnp.arange(blocks, dtype=jnp.int32)[:, None, None] * BLK + col_pos
    )
    visible = (col_pos <= row_pos + reach_rows) & (key_pos >= doc_begins[:, None, None])
    visible = visible[:, None, None]
    scores = (
        jnp.einsum("btgjd,bkgd->bgjtk", q_blocks, k_windows, preferred_element_type=jnp.float32)
        * score_scale
    )
    peak = jnp.max(jnp.where(visible, scores, -1e30), axis=-1, keepdims=True)
    weights = jnp.exp(jnp.where(visible, scores - peak, -1e30))
    probs = weights / jnp.sum(weights, axis=-1, keepdims=True)
    probs_b = probs.astype(jnp.bfloat16)
    outputs = jnp.einsum(
        "bgjtk,bkgd->btgjd", probs_b, v_windows, preferred_element_type=jnp.float32
    ).astype(jnp.bfloat16)
    deltas = jnp.sum(do_blocks.astype(jnp.float32) * outputs.astype(jnp.float32), axis=-1)
    dprobs = jnp.einsum(
        "btgjd,bkgd->bgjtk", do_blocks, v_windows, preferred_element_type=jnp.float32
    )
    dscores = (
        probs * (dprobs - jnp.transpose(deltas, (0, 2, 3, 1))[..., None]) * score_scale
    ).astype(jnp.bfloat16)
    d_queries = jnp.einsum(
        "bgjtk,bkgd->btgjd", dscores, k_windows, preferred_element_type=jnp.float32
    ).astype(jnp.bfloat16)
    dk_windows = jnp.einsum(
        "bgjtk,btgjd->bkgd", dscores, q_blocks, preferred_element_type=jnp.float32
    )
    dv_windows = jnp.einsum(
        "bgjtk,btgjd->bkgd", probs_b, do_blocks, preferred_element_type=jnp.float32
    )
    return (
        d_queries.reshape(blocks * BLK, -1),
        unwindowed(dk_windows, reach_rows, blocks).reshape(-1, kv_heads * HD),
        unwindowed(dv_windows, reach_rows, blocks).reshape(-1, kv_heads * HD),
    )


def per_device(query, key, value, d_out, doc_start):
    kv_key, kv_value = (
        lax.all_to_all(key, "head", split_axis=3, concat_axis=2, tiled=True),
        lax.all_to_all(value, "head", split_axis=3, concat_axis=2, tiled=True),
    )
    span_rows = kv_key.shape[2]
    ctx_index = lax.axis_index("ctx")
    ctx_count = lax.axis_size("ctx")
    is_last = ctx_index == ctx_count - 1
    rim_from = span_rows - span_rows
    outgoing = jnp.stack(
        [
            jnp.stack([kv_key[0, 1, rim_from:], kv_value[0, 1, rim_from:]]),
            jnp.stack([kv_key[0, 0, rim_from:], kv_value[0, 0, rim_from:]]),
        ]
    )
    incoming = padded_2(outgoing, (("ctx", 0),), 1)
    previous = [incoming[0], jnp.where(is_last, outgoing[1], incoming[3])]
    run_begin = (
        lax.cummax(
            jnp.where(doc_start == 1, jnp.arange(doc_start.shape[0], dtype=jnp.int32), 0), axis=0
        )
        * BLK
    )
    blocks = span_rows // BLK
    span_results = []
    for span_slot in range(2):
        span_id = ctx_index if span_slot == 0 else 2 * ctx_count - 1 - ctx_index
        span_start = span_id * span_rows
        doc_begins = lax.dynamic_slice_in_dim(run_begin, span_id * blocks, blocks)
        keys_ext = jnp.concatenate([previous[span_slot][0], kv_key[0, span_slot]], axis=0)
        values_ext = jnp.concatenate([previous[span_slot][1], kv_value[0, span_slot]], axis=0)
        span_results.append(
            span_grads(
                query[0, span_slot],
                d_out[0, span_slot],
                keys_ext,
                values_ext,
                doc_begins,
                span_start,
                span_rows,
            )
        )
    partials = jnp.stack(
        [
            jnp.stack([span_results[0][1][:span_rows], span_results[0][2][:span_rows]]),
            jnp.stack([span_results[1][1][:span_rows], span_results[1][2][:span_rows]]),
        ]
    )
    returned = padded_2(partials.astype(jnp.bfloat16), (("ctx", 0),), 1).astype(partials.dtype)
    added_parts = [returned[3] + jnp.where(is_last, partials[1], 0.0), returned[0]]
    key_grads = []
    value_grads = []
    for span_slot in range(2):
        own_key = (
            span_results[span_slot][1][span_rows:].at[rim_from:].add(added_parts[span_slot][0])
        )
        own_value = (
            span_results[span_slot][2][span_rows:].at[rim_from:].add(added_parts[span_slot][1])
        )
        key_grads.append(own_key.astype(jnp.bfloat16))
        value_grads.append(own_value.astype(jnp.bfloat16))
    d_query = jnp.stack([span_results[0][0], span_results[1][0]])[None]
    key_layout = jnp.stack(key_grads)[None]
    value_layout = jnp.stack(value_grads)[None]
    d_key, d_value = (
        lax.all_to_all(key_layout, "head", split_axis=2, concat_axis=3, tiled=True),
        lax.all_to_all(value_layout, "head", split_axis=2, concat_axis=3, tiled=True),
    )
    return (d_query, d_key, d_value)


def solution(mesh):
    return jax.shard_map(
        per_device,
        mesh=mesh,
        in_specs=(
            P("ctx", None, None, "head"),
            P("ctx", None, "head", None),
            P("ctx", None, "head", None),
            P("ctx", None, None, "head"),
            P(),
        ),
        out_specs=(
            P("ctx", None, None, "head"),
            P("ctx", None, "head", None),
            P("ctx", None, "head", None),
        ),
        check_vma=False,
    )
```

profile of v0, /device:TPU:26, one launch (start us, length us, event | category | flops | bytes accessed | tf_op | source)
XLA Modules:
  0.0 143.1 jit_solution(6247647339542804097)
XLA Ops:
  0.6 1.8 %copy.44 = bf16[1,2,128,512]{2,1,0,3:T(2,128)(2,1)} copy(bf16[1,2,128,512]{3,2,1,0:T(8,128)(2,1)} %param.22) | data formatting | bytes 524288 | tf_op args[1]
  2.5 4.8 %all-to-all-start = ((bf16[1,2,128,512]{2,1,0,3:T(2,128)(2,1)}), bf16[1,2,128,512]{2,1,0,3:T(2,128)(2,1)S(1)}, u32[]{:S(2)}, u32[]{:S(2)}) async-start(bf16[1,2,128,512]{2,1,0,3:T(2,128)(2,1)} %copy.44), calls=%async_computation | async-start | bytes 524288 | tf_op jit(solution)/shard_map/all_to_all | solution.py:100
  8.6 1.8 %copy.46 = bf16[1,2,128,512]{2,1,0,3:T(2,128)(2,1)} copy(bf16[1,2,128,512]{3,2,1,0:T(8,128)(2,1)} %param.23) | data formatting | bytes 524288 | tf_op args[2]
  10.4 1.7 %slice_bitcast_fusion.1 = (bf16[64,8,8,128]{3,1,2,0:T(8,128)(2,1)S(1)}, bf16[64,8,8,128]{3,1,2,0:T(8,128)(2,1)S(1)}) fusion(bf16[1,2,512,1024]{3,2,1,0:T(8,128)(2,1)} %param.21), kind=kLoop, calls=%fused_computation.56 | loop fusion | bytes 4194304
  12.1 4.6 %slice_bitcast_fusion.3 = (bf16[64,8,8,128]{3,1,2,0:T(8,128)(2,1)}, f32[64,8,8,128]{3,1,2,0:T(8,128)}, f32[64,8,8,128]{3,1,2,0:T(8,128)}, bf16[64,8,8,128]{3,1,2,0:T(8,128)(2,1)}) fusion(bf16[1,2,512,1024]{3,2,1,0:T(8,128)(2,1)} %param.24), kind=kLoop, calls=%fused_computation.68 | loop fusion | flops 1048576 | bytes 8388608
  16.9 4.8 %all-to-all-start.1 = ((bf16[1,2,128,512]{2,1,0,3:T(2,128)(2,1)}), bf16[1,2,128,512]{2,1,0,3:T(2,128)(2,1)S(1)}, u32[]{:S(2)}, u32[]{:S(2)}) async-start(bf16[1,2,128,512]{2,1,0,3:T(2,128)(2,1)} %copy.46), calls=%async_computation.1 | async-start | bytes 524288 | tf_op jit(solution)/shard_map/all_to_all | solution.py:101
  22.5 4.3 %all-to-all-done.1 = bf16[1,2,128,512]{2,1,0,3:T(2,128)(2,1)S(1)} async-done(((bf16[1,2,128,512]{2,1,0,3:T(2,128)(2,1)}), bf16[1,2,128,512]{2,1,0,3:T(2,128)(2,1)S(1)}, u32[]{:S(2)}, u32[]{:S(2)}) %all-to-all-start.1) | async-done | bytes 262176 | tf_op jit(solution)/shard_map/all_to_all | solution.py:101
  27.1 1.0 fusion.102
  28.8 5.4 %collective-permute-start.1 = (bf16[1,2,512,128]{3,2,1,0:T(8,128)(2,1)}, bf16[1,2,512,128]{3,2,1,0:T(8,128)(2,1)}, u32[]{:S(2)}, u32[]{:S(2)}) collective-permute-start(bf16[1,2,512,128]{3,2,1,0:T(8,128)(2,1)} %maximum_bitcast_fusion.1), channel_id=1, source_target_pairs={{4,0},{8,4},{12,8},{16,12},{20,16},{24,20},{28,24},{32,28},{36,32}... | collective-permute-start | bytes 786440 | tf_op jit(solution)/shard_map/ppermute | solution.py:21
  34.8 2.5 %copy.98 = bf16[64,8,8,128]{3,2,1,0:T(8,128)(2,1)} copy(bf16[64,8,8,128]{3,1,2,0:T(8,128)(2,1)} %get-tuple-element.83) | data formatting | bytes 2097152
  37.3 1.5 %copy.101 = bf16[64,8,8,128]{3,2,1,0:T(8,128)(2,1)S(1)} copy(bf16[64,8,8,128]{3,1,2,0:T(8,128)(2,1)} %get-tuple-element.86) | data formatting | bytes 2097152
  38.8 3.4 %copy.99 = f32[64,8,8,128]{3,2,1,0:T(8,128)} copy(f32[64,8,8,128]{3,1,2,0:T(8,128)} %get-tuple-element.84) | data formatting | bytes 4194304
  42.2 2.9 %copy.52 = f32[4,128,1,8,128]{1,4,3,0,2:T(8,128)} copy(f32[4,128,1,8,128]{4,3,2,1,0:T(8,128)} %bitcast.414) | data formatting | bytes 4194304 | tf_op jit(solution)/shard_map/convert_element_type | solution.py:75
  45.1 3.4 %copy.102 = f32[64,8,8,128]{3,2,1,0:T(8,128)} copy(f32[64,8,8,128]{3,1,2,0:T(8,128)} %get-tuple-element.85) | data formatting | bytes 4194304
  48.5 2.9 %copy.60 = f32[4,128,1,8,128]{1,4,3,0,2:T(8,128)} copy(f32[4,128,1,8,128]{4,3,2,1,0:T(8,128)} %bitcast.415) | data formatting | bytes 4194304 | tf_op jit(solution)/shard_map/convert_element_type | solution.py:75
  51.4 2.2 %broadcast_and_fusion.1 = (pred[4,128,640]{1,2,0:T(8,128)(4,1)S(1)}, pred[4,128,640]{1,2,0:T(8,128)(4,1)S(1)}) fusion(pred[4,640]{1,0:T(4,128)(4,1)S(1)} %get-tuple-element.162, pred[128,640]{0,1:T(8,128)(4,1)} %iota_compare_fusion, pred[4,640]{1,0:T(4,128)(4,1)S(1)} %get-tuple-element.161), kind=kLoop, calls=%fused_computation.78 | loop fusion | flops 655360 | bytes 742400 | tf_op jit(solution)/shard_map/and | solution.py:62
  53.6 1.8 %fusion.81 = (bf16[1,2,512,128]{3,2,1,0:T(8,128)(2,1)}, bf16[2,512,128]{2,1,0:T(8,128)(2,1)S(1)}) fusion(bf16[1,512,128]{2,1,0:T(8,128)(2,1)} %get-tuple-element.159, bf16[1,512,128]{2,1,0:T(8,128)(2,1)} %get-tuple-element.114, bf16[1,2,512,128]{3,2,1,0:T(8,128)(2,1)} %collective-permute-done.1, pred[]{:T(512)S(6)} %eq.11), kind=kLoop, calls=%fused_computation.125 | loop fusion | flops 262144 | bytes 1048577 | tf_op jit(solution)/shard_map/stack | solution.py:108
  55.4 2.1 %collective-permute-start = (bf16[1,2,512,128]{3,2,1,0:T(8,128)(2,1)}, bf16[1,2,512,128]{3,2,1,0:T(8,128)(2,1)}, u32[]{:S(2)}, u32[]{:S(2)}) collective-permute-start(bf16[1,2,512,128]{3,2,1,0:T(8,128)(2,1)} %get-tuple-element.135), channel_id=1, source_target_pairs={{0,4},{4,8},{8,12},{12,16},{16,20},{20,24},{24,28},{28,32},{32,36}... | collective-permute-start | bytes 786440 | tf_op jit(solution)/shard_map/ppermute | solution.py:19
  58.9 1.6 %fusion.6 = (f32[4,8,128]{2,1,0:T(8,128)S(1)}, f32[4,640,128,8]{2,1,3,0:T(8,128)S(1)}) fusion(pred[4,128,640]{1,2,0:T(8,128)(4,1)S(1)} %get-tuple-element.148, bf16[4,128,8,128]{3,2,1,0:T(8,128)(2,1)S(1)} %bitcast.412, bf16[4,640,1,128]{3,1,0,2:T(8,128)(2,1)S(1)} %constant_dynamic-update-slice_fusion.10), kind=kOutput, calls=%fused_computation.10 | convolution fusion | flops 678948864 | bytes 12533760 | tf_op jit(solution)/shard_map/btgjd,bkgd->bgjtk/dot_general | solution.py:65
  60.5 2.4 %fusion.15 = f32[4,8,128]{2,1,0:T(8,128)S(1)} fusion(f32[4,640,128,8]{2,1,3,0:T(8,128)S(1)} %get-tuple-element.152, f32[4,8,128]{2,1,0:T(8,128)S(1)} %get-tuple-element.151, pred[4,128,640]{1,2,0:T(8,128)(4,1)S(1)} %get-tuple-element.148), kind=kLoop, calls=%fused_computation.21 | loop fusion | flops 10481664 | bytes 10846208 | tf_op jit(solution)/shard_map/reduce_sum | solution.py:70
  62.9 3.1 %fusion.41 = f32[4,640,1,128]{3,1,0,2:T(8,128)S(1)} fusion(bf16[4,128,8,128]{3,2,1,0:T(8,128)(2,1)S(1)} %bitcast.439, f32[4,8,128]{2,1,0:T(8,128)S(1)} %fusion.15, f32[4,8,128]{2,1,0:T(8,128)S(1)} %get-tuple-element.151, f32[4,640,128,8]{2,1,3,0:T(8,128)S(1)} %get-tuple-element.152, pred[4,128,640]{1,2,0:T(8,128)(4,1)S(1)} %get-tuple-element.148), kind=kOutput, calls=%fused_computation.50 | convolution fusion | flops 684195840 | bytes 13205504 | tf_op jit(solution)/shard_map/bgjtk,btgjd->bkgd/dot_general | solution.py:88
  66.1 3.2 %fusion.29 = f32[4,128,8]{1,2,0:T(8,128)S(1)} fusion(f32[4,128,1,8,128]{1,4,3,0,2:T(8,128)S(1)} %copy-done.6, bf16[4,640,1,128]{3,1,0,2:T(8,128)(2,1)S(1)} %constant_dynamic-update-slice_fusion.15, f32[4,8,128]{2,1,0:T(8,128)S(1)} %fusion.15, f32[4,8,128]{2,1,0:T(8,128)S(1)} %get-tuple-element.151, f32[4,640,128,8]{2,1,3,0:T(8,128)S(1)} %get-tuple-element.152, ...), kind=kOutput, calls=%fused_computation.37 | convolution fusion | flops 686288896 | bytes 13615104 | tf_op jit(solution)/shard_map/bgjtk,bkgd->btgjd/dot_general | solution.py:72
  69.2 4.2 %fusion.17 = bf16[4,8,128,640]{2,3,1,0:T(8,128)(2,1)S(1)} fusion(f32[4,8,128]{2,1,0:T(8,128)S(1)} %bitcast.468, f32[4,8,128]{2,1,0:T(8,128)S(1)} %fusion.15, f32[4,8,128]{2,1,0:T(8,128)S(1)} %get-tuple-element.151, f32[4,640,128,8]{2,1,3,0:T(8,128)S(1)} %get-tuple-element.152, pred[4,128,640]{1,2,0:T(8,128)(4,1)S(1)} %get-tuple-element.148, ...), kind=kOutput, calls=%fused_computation.23 | convolution fusion | flops 692060160 | bytes 17809408 | tf_op jit(solution)/shard_map/btgjd,bkgd->bgjtk/dot_general | solution.py:76
  73.6 1.5 %convolution_bitcast_fusion = f32[4,640,1,128]{3,1,0,2:T(8,128)S(1)} fusion(bf16[4,8,128,640]{2,3,1,0:T(8,128)(2,1)S(1)} %fusion.17, bf16[4,128,8,128]{3,2,1,0:T(8,128)(2,1)S(1)} %bitcast.413), kind=kOutput, calls=%fused_computation.47 | convolution fusion | flops 671088640 | bytes 7602176 | tf_op jit(solution)/shard_map/bgjtk,btgjd->bkgd/dot_general | solution.py:85
  76.2 2.1 %collective-permute-start.2 = (bf16[1,2,512,128]{3,2,1,0:T(8,128)(2,1)S(1)}, bf16[1,2,512,128]{3,2,1,0:T(8,128)(2,1)S(1)}, u32[]{:S(2)}, u32[]{:S(2)}) collective-permute-start(bf16[1,2,512,128]{3,2,1,0:T(8,128)(2,1)S(1)} %fusion.76), channel_id=1, source_target_pairs={{0,4},{4,8},{8,12},{12,16},{16,20},{20,24},{24,28},{28,32},{32,36}... | collective-permute-start | bytes 786440 | tf_op jit(solution)/shard_map/ppermute | solution.py:19
  78.4 1.0 slice_bitcast_fusion.12
  79.9 1.6 %fusion.9 = (f32[4,8,128]{2,1,0:T(8,128)S(1)}, f32[4,640,128,8]{2,1,3,0:T(8,128)S(1)}) fusion(pred[4,128,640]{1,2,0:T(8,128)(4,1)S(1)} %get-tuple-element.147, bf16[4,128,8,128]{3,2,1,0:T(8,128)(2,1)S(1)} %bitcast.410, bf16[4,640,1,128]{3,1,0,2:T(8,128)(2,1)S(1)} %constant_dynamic-update-slice_fusion), kind=kOutput, calls=%fused_computation.15 | convolution fusion | flops 678948864 | bytes 12533760 | tf_op jit(solution)/shard_map/btgjd,bkgd->bgjtk/dot_general | solution.py:65
  81.5 2.4 %fusion.13 = f32[4,8,128]{2,1,0:T(8,128)S(1)} fusion(f32[4,640,128,8]{2,1,3,0:T(8,128)S(1)} %get-tuple-element.154, f32[4,8,128]{2,1,0:T(8,128)S(1)} %get-tuple-element.153, pred[4,128,640]{1,2,0:T(8,128)(4,1)S(1)} %get-tuple-element.147), kind=kLoop, calls=%fused_computation.19 | loop fusion | flops 10481664 | bytes 10846208 | tf_op jit(solution)/shard_map/reduce_sum | solution.py:70
  83.9 4.2 %fusion.38 = f32[4,640,1,128]{3,1,0,2:T(8,128)S(1)} fusion(bf16[4,128,8,128]{3,2,1,0:T(8,128)(2,1)} %bitcast.437, f32[4,8,128]{2,1,0:T(8,128)S(1)} %fusion.13, f32[4,8,128]{2,1,0:T(8,128)S(1)} %get-tuple-element.153, f32[4,640,128,8]{2,1,3,0:T(8,128)S(1)} %get-tuple-element.154, pred[4,128,640]{1,2,0:T(8,128)(4,1)S(1)} %get-tuple-element.147), kind=kOutput, calls=%fused_computation.49 | convolution fusion | flops 684195840 | bytes 13205504 | tf_op jit(solution)/shard_map/bgjtk,btgjd->bkgd/dot_general | solution.py:88
  88.2 4.4 %fusion.31 = f32[4,128,8]{1,2,0:T(8,128)S(1)} fusion(f32[4,128,1,8,128]{1,4,3,0,2:T(8,128)S(1)} %copy-done.5, bf16[4,640,1,128]{3,1,0,2:T(8,128)(2,1)} %copy-done.14, f32[4,8,128]{2,1,0:T(8,128)S(1)} %fusion.13, f32[4,8,128]{2,1,0:T(8,128)S(1)} %get-tuple-element.153, f32[4,640,128,8]{2,1,3,0:T(8,128)S(1)} %get-tuple-element.154, ...), kind=kOutput, calls=%fused_computation.40 | convolution fusion | flops 686288896 | bytes 13615104 | tf_op jit(solution)/shard_map/bgjtk,bkgd->btgjd/dot_general | solution.py:72
  92.6 4.2 %fusion.16 = bf16[4,8,128,640]{2,3,1,0:T(8,128)(2,1)S(1)} fusion(f32[4,8,128]{2,1,0:T(8,128)S(1)} %bitcast.469, f32[4,8,128]{2,1,0:T(8,128)S(1)} %fusion.13, f32[4,8,128]{2,1,0:T(8,128)S(1)} %get-tuple-element.153, f32[4,640,128,8]{2,1,3,0:T(8,128)S(1)} %get-tuple-element.154, pred[4,128,640]{1,2,0:T(8,128)(4,1)S(1)} %get-tuple-element.147, ...), kind=kOutput, calls=%fused_computation.22 | convolution fusion | flops 692060160 | bytes 17809408 | tf_op jit(solution)/shard_map/btgjd,bkgd->bgjtk/dot_general | solution.py:76
  97.0 2.1 %copy-done = bf16[4,8,128,640]{2,3,1,0:T(8,128)(2,1)} copy-done((bf16[4,8,128,640]{2,3,1,0:T(8,128)(2,1)}, bf16[4,8,128,640]{2,3,1,0:T(8,128)(2,1)S(1)}, u32[]{:S(2)}) %copy-start) | copy-done | bytes 5242904
  99.1 1.5 %convolution_bitcast_fusion.1 = f32[4,640,1,128]{3,1,0,2:T(8,128)S(1)} fusion(bf16[4,8,128,640]{2,3,1,0:T(8,128)(2,1)S(1)} %fusion.16, bf16[4,128,8,128]{3,2,1,0:T(8,128)(2,1)S(1)} %bitcast.411), kind=kOutput, calls=%fused_computation.48 | convolution fusion | flops 671088640 | bytes 7602176 | tf_op jit(solution)/shard_map/bgjtk,btgjd->bkgd/dot_general | solution.py:85
  101.7 6.0 %collective-permute-start.3 = (bf16[1,2,512,128]{3,2,1,0:T(8,128)(2,1)S(1)}, bf16[1,2,512,128]{3,2,1,0:T(8,128)(2,1)S(1)}, u32[]{:S(2)}, u32[]{:S(2)}) collective-permute-start(bf16[1,2,512,128]{3,2,1,0:T(8,128)(2,1)S(1)} %maximum_bitcast_fusion.2), channel_id=1, source_target_pairs={{4,0},{8,4},{12,8},{16,12},{20,16},{24,20},{28,24},{32,28},{36,32}... | collective-permute-start | bytes 786440 | tf_op jit(solution)/shard_map/ppermute | solution.py:21
  107.7 2.0 %fusion.45 = bf16[4,128,1,8,128]{1,4,3,0,2:T(8,128)(2,1)} fusion(bf16[4,8,128,640]{2,3,1,0:T(8,128)(2,1)S(1)} %fusion.17, bf16[4,640,1,128]{3,1,0,2:T(8,128)(2,1)S(1)} %constant_dynamic-update-slice_fusion.10), kind=kOutput, calls=%fused_computation.52 | convolution fusion | flops 671612928 | bytes 6946816 | tf_op jit(solution)/shard_map/bgjtk,bkgd->btgjd/dot_general | solution.py:82
  109.7 1.7 %copy.63 = bf16[4,128,1,8,128]{4,3,1,0,2:T(8,128)(2,1)S(1)} copy(bf16[4,128,1,8,128]{1,4,3,0,2:T(8,128)(2,1)} %fusion.45) | data formatting | bytes 2097152 | tf_op jit(solution)/shard_map/convert_element_type | solution.py:84
  111.4 1.3 stack_reshape.7
  112.8 1.2 fusion.79
  113.9 1.0 fusion.78
  115.9 4.8 %all-to-all-start.3 = ((bf16[1,2,512,128]{3,1,0,2:T(2,128)(2,1)}), bf16[1,2,512,128]{3,1,0,2:T(2,128)(2,1)S(1)}, u32[]{:S(2)}, u32[]{:S(2)}) async-start(bf16[1,2,512,128]{3,1,0,2:T(2,128)(2,1)} %copy.71), calls=%async_computation.3 | async-start | bytes 524288 | tf_op jit(solution)/shard_map/all_to_all | solution.py:165
  120.8 1.2 add_convert_fusion
  122.2 1.3 maximum_bitcast_fusion.3
  123.5 2.5 %all-to-all-done.3 = bf16[1,2,512,128]{3,1,0,2:T(2,128)(2,1)S(1)} async-done(((bf16[1,2,512,128]{3,1,0,2:T(2,128)(2,1)}), bf16[1,2,512,128]{3,1,0,2:T(2,128)(2,1)S(1)}, u32[]{:S(2)}, u32[]{:S(2)}) %all-to-all-start.3) | async-done | bytes 262176 | tf_op jit(solution)/shard_map/all_to_all | solution.py:165
  126.0 4.8 %all-to-all-start.2 = ((bf16[1,2,512,128]{3,1,0,2:T(2,128)(2,1)}), bf16[1,2,512,128]{3,1,0,2:T(2,128)(2,1)S(1)}, u32[]{:S(2)}, u32[]{:S(2)}) async-start(bf16[1,2,512,128]{3,1,0,2:T(2,128)(2,1)} %maximum_bitcast_fusion.3), calls=%async_computation.2 | async-start | bytes 524288 | tf_op jit(solution)/shard_map/all_to_all | solution.py:164
  130.8 4.5 %fusion.44 = bf16[4,128,1,8,128]{1,4,3,0,2:T(8,128)(2,1)} fusion(bf16[4,8,128,640]{2,3,1,0:T(8,128)(2,1)} %copy-done, bf16[4,640,1,128]{3,1,0,2:T(8,128)(2,1)S(1)} %constant_dynamic-update-slice_fusion), kind=kOutput, calls=%fused_computation.51 | convolution fusion | flops 671612928 | bytes 6946816 | tf_op jit(solution)/shard_map/bgjtk,bkgd->btgjd/dot_general | solution.py:82
  135.4 1.7 %copy.55 = bf16[4,128,1,8,128]{4,3,1,0,2:T(8,128)(2,1)S(1)} copy(bf16[4,128,1,8,128]{1,4,3,0,2:T(8,128)(2,1)} %fusion.44) | data formatting | bytes 2097152 | tf_op jit(solution)/shard_map/convert_element_type | solution.py:84
  137.0 1.3 stack_reshape.6
  138.3 2.7 %maximum_bitcast_fusion = bf16[1,2,512,1024]{3,2,1,0:T(8,128)(2,1)} fusion(bf16[1,512,1024]{2,1,0:T(8,128)(2,1)S(1)} %copy-done.1, bf16[1,512,1024]{2,1,0:T(8,128)(2,1)} %stack_reshape.6), kind=kLoop, calls=%fused_computation.34 | loop fusion | flops 1048576 | bytes 4194304 | tf_op jit(solution)/shard_map/broadcast_in_dim | solution.py:160
  (102 shorter events, 11.1 us)
Async XLA Ops:
  2.5 14.4 %all-to-all-start = ((bf16[1,2,128,512]{2,1,0,3:T(2,128)(2,1)}), bf16[1,2,128,512]{2,1,0,3:T(2,128)(2,1)S(1)}, u32[]{:S(2)}, u32[]{:S(2)}) async-start(bf16[1,2,128,512]{2,1,0,3:T(2,128)(2,1)} %copy.44), calls=%async_computation | async-start | bytes 524288 | tf_op jit(solution)/shard_map/all_to_all | solution.py:100
  16.9 10.0 %all-to-all-start.1 = ((bf16[1,2,128,512]{2,1,0,3:T(2,128)(2,1)}), bf16[1,2,128,512]{2,1,0,3:T(2,128)(2,1)S(1)}, u32[]{:S(2)}, u32[]{:S(2)}) async-start(bf16[1,2,128,512]{2,1,0,3:T(2,128)(2,1)} %copy.46), calls=%async_computation.1 | async-start | bytes 524288 | tf_op jit(solution)/shard_map/all_to_all | solution.py:101
  28.8 24.8 %collective-permute-start.1 = (bf16[1,2,512,128]{3,2,1,0:T(8,128)(2,1)}, bf16[1,2,512,128]{3,2,1,0:T(8,128)(2,1)}, u32[]{:S(2)}, u32[]{:S(2)}) collective-permute-start(bf16[1,2,512,128]{3,2,1,0:T(8,128)(2,1)} %maximum_bitcast_fusion.1), channel_id=1, source_target_pairs={{4,0},{8,4},{12,8},{16,12},{20,16},{24,20},{28,24},{32,28},{36,32}... | collective-permute-start | bytes 786440 | tf_op jit(solution)/shard_map/ppermute | solution.py:21
  55.4 23.0 %collective-permute-start = (bf16[1,2,512,128]{3,2,1,0:T(8,128)(2,1)}, bf16[1,2,512,128]{3,2,1,0:T(8,128)(2,1)}, u32[]{:S(2)}, u32[]{:S(2)}) collective-permute-start(bf16[1,2,512,128]{3,2,1,0:T(8,128)(2,1)} %get-tuple-element.135), channel_id=1, source_target_pairs={{0,4},{4,8},{8,12},{12,16},{16,20},{20,24},{24,28},{28,32},{32,36}... | collective-permute-start | bytes 786440 | tf_op jit(solution)/shard_map/ppermute | solution.py:19
  62.9 3.1 %copy-start.6 = (f32[4,128,1,8,128]{1,4,3,0,2:T(8,128)S(1)}, f32[4,128,1,8,128]{1,4,3,0,2:T(8,128)}, u32[]{:S(2)}) copy-start(f32[4,128,1,8,128]{1,4,3,0,2:T(8,128)} %copy.60) | copy-start | bytes 6291460
  73.5 6.0 %copy-start.11 = (bf16[512,128]{1,0:T(8,128)(2,1)S(1)}, bf16[512,128]{1,0:T(8,128)(2,1)}, u32[]{:S(2)}) copy-start(bf16[512,128]{1,0:T(8,128)(2,1)} %get-tuple-element.115) | copy-start | bytes 393220
  73.5 6.1 %copy-start.10 = (bf16[512,128]{1,0:T(8,128)(2,1)S(1)}, bf16[512,128]{1,0:T(8,128)(2,1)}, u32[]{:S(2)}) copy-start(bf16[512,128]{1,0:T(8,128)(2,1)} %get-tuple-element.158) | copy-start | bytes 393220
  73.6 6.1 %copy-start.13 = (bf16[1,1,512,128]{3,2,1,0:T(8,128)(2,1)S(1)}, bf16[1,1,512,128]{3,2,1,0:T(8,128)(2,1)}, u32[]{:S(2)}) copy-start(bf16[1,1,512,128]{3,2,1,0:T(8,128)(2,1)} %get-tuple-element.160) | copy-start | bytes 393220
  73.6 6.2 %copy-start.12 = (bf16[1,1,512,128]{3,2,1,0:T(8,128)(2,1)S(1)}, bf16[1,1,512,128]{3,2,1,0:T(8,128)(2,1)}, u32[]{:S(2)}) copy-start(bf16[1,1,512,128]{3,2,1,0:T(8,128)(2,1)} %get-tuple-element.113) | copy-start | bytes 393220
  76.1 5.4 %copy-start.2 = (f32[1,512,128]{2,1,0:T(8,128)}, f32[1,512,128]{2,1,0:T(8,128)S(1)}, u32[]{:S(2)}) copy-start(f32[1,512,128]{2,1,0:T(8,128)S(1)} %get-tuple-element.111) | copy-start | bytes 786436
  76.2 5.4 %copy-start.4 = (f32[1024,1,128]{2,0,1:T(8,128)}, f32[1024,1,128]{2,0,1:T(8,128)S(1)}, u32[]{:S(2)}) copy-start(f32[1024,1,128]{2,0,1:T(8,128)S(1)} %pad_add_fusion.1) | copy-start | bytes 1572868
  76.2 36.5 %collective-permute-start.2 = (bf16[1,2,512,128]{3,2,1,0:T(8,128)(2,1)S(1)}, bf16[1,2,512,128]{3,2,1,0:T(8,128)(2,1)S(1)}, u32[]{:S(2)}, u32[]{:S(2)}) collective-permute-start(bf16[1,2,512,128]{3,2,1,0:T(8,128)(2,1)S(1)} %fusion.76), channel_id=1, source_target_pairs={{0,4},{4,8},{8,12},{12,16},{16,20},{20,24},{24,28},{28,32},{32,36}... | collective-permute-start | bytes 786440 | tf_op jit(solution)/shard_map/ppermute | solution.py:19
  79.7 4.2 %copy-start.14 = (bf16[4,640,1,128]{3,1,0,2:T(8,128)(2,1)}, bf16[4,640,1,128]{3,1,0,2:T(8,128)(2,1)S(1)}, u32[]{:S(2)}) copy-start(bf16[4,640,1,128]{3,1,0,2:T(8,128)(2,1)S(1)} %constant_dynamic-update-slice_fusion.5) | copy-start | bytes 1966084
  83.9 4.2 %copy-start.5 = (f32[4,128,1,8,128]{1,4,3,0,2:T(8,128)S(1)}, f32[4,128,1,8,128]{1,4,3,0,2:T(8,128)}, u32[]{:S(2)}) copy-start(f32[4,128,1,8,128]{1,4,3,0,2:T(8,128)} %copy.52) | copy-start | bytes 6291460
  88.2 4.4 %copy-start.9 = (bf16[64,8,8,128]{3,2,1,0:T(8,128)(2,1)S(1)}, bf16[64,8,8,128]{3,2,1,0:T(8,128)(2,1)}, u32[]{:S(2)}) copy-start(bf16[64,8,8,128]{3,2,1,0:T(8,128)(2,1)} %copy.98) | copy-start | bytes 3145732
  88.2 4.4 %copy-start.15 = (bf16[4,640,1,128]{3,1,0,2:T(8,128)(2,1)S(1)}, bf16[4,640,1,128]{3,1,0,2:T(8,128)(2,1)}, u32[]{:S(2)}) copy-start(bf16[4,640,1,128]{3,1,0,2:T(8,128)(2,1)} %copy-done.14) | copy-start | bytes 1966084
  96.8 2.3 %copy-start = (bf16[4,8,128,640]{2,3,1,0:T(8,128)(2,1)}, bf16[4,8,128,640]{2,3,1,0:T(8,128)(2,1)S(1)}, u32[]{:S(2)}) copy-start(bf16[4,8,128,640]{2,3,1,0:T(8,128)(2,1)S(1)} %fusion.16) | copy-start | bytes 15728644
  97.0 10.7 %copy-start.7 = (f32[1024,1,128]{2,0,1:T(8,128)}, f32[1024,1,128]{2,0,1:T(8,128)S(1)}, u32[]{:S(2)}) copy-start(f32[1024,1,128]{2,0,1:T(8,128)S(1)} %pad_add_fusion) | copy-start | bytes 1572868
  100.7 12.0 %copy-start.3 = (f32[1,512,128]{2,1,0:T(8,128)S(1)}, f32[1,512,128]{2,1,0:T(8,128)}, u32[]{:S(2)}) copy-start(f32[1,512,128]{2,1,0:T(8,128)} %copy-done.2) | copy-start | bytes 786436
  100.9 0.8 copy-start.8
  101.7 11.0 %collective-permute-start.3 = (bf16[1,2,512,128]{3,2,1,0:T(8,128)(2,1)S(1)}, bf16[1,2,512,128]{3,2,1,0:T(8,128)(2,1)S(1)}, u32[]{:S(2)}, u32[]{:S(2)}) collective-permute-start(bf16[1,2,512,128]{3,2,1,0:T(8,128)(2,1)S(1)} %maximum_bitcast_fusion.2), channel_id=1, source_target_pairs={{4,0},{8,4},{12,8},{16,12},{20,16},{24,20},{28,24},{32,28},{36,32}... | collective-permute-start | bytes 786440 | tf_op jit(solution)/shard_map/ppermute | solution.py:21
  112.7 25.6 %copy-start.1 = (bf16[1,512,1024]{2,1,0:T(8,128)(2,1)S(1)}, bf16[1,512,1024]{2,1,0:T(8,128)(2,1)}, u32[]{:S(2)}) copy-start(bf16[1,512,1024]{2,1,0:T(8,128)(2,1)} %stack_reshape.7) | copy-start | bytes 3145732
  115.9 10.1 %all-to-all-start.3 = ((bf16[1,2,512,128]{3,1,0,2:T(2,128)(2,1)}), bf16[1,2,512,128]{3,1,0,2:T(2,128)(2,1)S(1)}, u32[]{:S(2)}, u32[]{:S(2)}) async-start(bf16[1,2,512,128]{3,1,0,2:T(2,128)(2,1)} %copy.71), calls=%async_computation.3 | async-start | bytes 524288 | tf_op jit(solution)/shard_map/all_to_all | solution.py:165
  126.0 16.1 %all-to-all-start.2 = ((bf16[1,2,512,128]{3,1,0,2:T(2,128)(2,1)}), bf16[1,2,512,128]{3,1,0,2:T(2,128)(2,1)S(1)}, u32[]{:S(2)}, u32[]{:S(2)}) async-start(bf16[1,2,512,128]{3,1,0,2:T(2,128)(2,1)} %maximum_bitcast_fusion.3), calls=%async_computation.2 | async-start | bytes 524288 | tf_op jit(solution)/shard_map/all_to_all | solution.py:164
where the time goes:
time: 144 us; the launch traced here: 143 us
  local copies, waits for them, and re-layouts  39.7 us (28%)
  matrix products  36.2 us (25%)
  starting transfers between devices  34.9 us (24%)
  other arithmetic  24.1 us (17%)
  waiting for transfers between devices  6.8 us (5%)
    unnamed x57, local copies, waits for them, and re-layouts  19.9 us
    ppermute x2, starting transfers between devices, padded_2(): lax.ppermute(head, axis, [((i + 1) % count, i) for i in range(ends)])  11.4 us
    dot_general x2, matrix products, span_grads(): jnp.einsum('btgjd,bkgd->bgjtk', do_blocks, v_windows, preferred_element_t...  8.42 us
    dot_general x2, matrix products, span_grads(): jnp.einsum('bgjtk,bkgd->btgjd', probs_b, v_windows, preferred_element_typ...  7.54 us
    dot_general x2, matrix products, span_grads(): jnp.einsum('bgjtk,btgjd->bkgd', probs_b, do_blocks, preferred_element_typ...  7.32 us
    dot_general x2, matrix products, span_grads(): jnp.einsum('bgjtk,bkgd->btgjd', dscores, k_windows, preferred_element_typ...  6.55 us
    convert_element_type x2, local copies, waits for them, and re-layouts, span_grads(): do_blocks.astype(jnp.float32) * outputs.astype(jnp.float32)  5.78 us
    all_to_all x1, starting transfers between devices, per_device(): lax.all_to_all(value_layout, 'head', split_axis=2, concat_axis=3, tiled=T...  4.84 us
  transfers between devices with their start and end apart: 8, of which 2 were waited for; matrix products, arithmetic and copies ran while one was open for 60% of the time, Pallas kernels for 0%

commit v1 on v0

--- a/solution.py
+++ b/solution.py
@@ -97,7 +97,10 @@
 
 def per_device(query, key, value, d_out, doc_start):
     kv_key, kv_value = (
-        lax.all_to_all(key, "head", split_axis=3, concat_axis=2, tiled=True),
+        jnp.concatenate(
+            lax.all_to_all(jnp.stack(jnp.split(key, lax.axis_size("head"), axis=3)), "head", 0, 0),
+            axis=2,
+        ),
         lax.all_to_all(value, "head", split_axis=3, concat_axis=2, tiled=True),
     )
     span_rows = kv_key.shape[2]

time: 144 us -> 134 us (0.931)
  other arithmetic: 24.1 us -> 18.5 us
  local copies, waits for them, and re-layouts: 39.7 us -> 34.3 us
    all_to_all x1, waiting for transfers between devices: 4.33 us -> 0.01 us  [per_device(): lax.all_to_all(value, 'head', split_axis=3, concat_axis=2, tiled=True)]
    all_to_all x1, waiting for transfers between devices: 0.01 us -> 4.33 us  [per_device(): lax.all_to_all(jnp.stack(jnp.split(key, lax.axis_size('head'), axis=3)),...]
    ppermute x2, waiting for transfers between devices: 0.01 us -> 3.86 us  [padded_2(): lax.ppermute(head, axis, [((i + 1) % count, i) for i in range(ends)])]
    unnamed x57 -> x52, local copies, waits for them, and re-layouts: 19.9 us -> 16.3 us
    dot_general x2, matrix products: 6.55 us -> 9.01 us  [span_grads(): jnp.einsum('bgjtk,bkgd->btgjd', dscores, k_windows, preferred_element_typ...]
    all_to_all x1, waiting for transfers between devices: 2.45 us -> 0.01 us  [per_device(): lax.all_to_all(value_layout, 'head', split_axis=2, concat_axis=3, tiled=T...]
    convert_element_type x2, other arithmetic: 2.15 us -> 0.16 us  [per_device(): value_grads.append(own_value.astype(jnp.bfloat16))]
  transfers between devices with their start and end apart: 8 -> 8, of which waited for: 2 -> 2; matrix products, arithmetic and copies ran while one was open for 60% -> 61% of each run, Pallas kernels for 0% -> 0%
where the time goes in v1:
time: 134 us; the launch traced here: 133 us
  matrix products  36.4 us (27%)
  starting transfers between devices  34.6 us (26%)
  local copies, waits for them, and re-layouts  34.3 us (26%)
  other arithmetic  18.5 us (14%)
  waiting for transfers between devices  8.2 us (6%)
  between operations  1.38 us (1%)
    unnamed x52, local copies, waits for them, and re-layouts  16.3 us
    ppermute x2, starting transfers between devices, padded_2(): lax.ppermute(head, axis, [((i + 1) % count, i) for i in range(ends)])  11.1 us
    dot_general x2, matrix products, span_grads(): jnp.einsum('bgjtk,bkgd->btgjd', dscores, k_windows, preferred_element_typ...  9.01 us
    dot_general x2, matrix products, span_grads(): jnp.einsum('btgjd,bkgd->bgjtk', do_blocks, v_windows, preferred_element_t...  8.43 us
    dot_general x2, matrix products, span_grads(): jnp.einsum('bgjtk,bkgd->btgjd', probs_b, v_windows, preferred_element_typ...  6.34 us
    dot_general x2, matrix products, span_grads(): jnp.einsum('bgjtk,btgjd->bkgd', probs_b, do_blocks, preferred_element_typ...  6.25 us
    convert_element_type x2, local copies, waits for them, and re-layouts, span_grads(): do_blocks.astype(jnp.float32) * outputs.astype(jnp.float32)  5.85 us
    reduce_sum x2, other arithmetic, span_grads(): probs = weights / jnp.sum(weights, axis=-1, keepdims=True)  4.89 us
  transfers between devices with their start and end apart: 8, of which 2 were waited for; matrix products, arithmetic and copies ran while one was open for 61% of the time, Pallas kernels for 0%

profile of v1, /device:TPU:26, one launch (start us, length us, event | category | flops | bytes accessed | tf_op | source)
XLA Modules:
  0.0 133.4 jit_solution(2179701548588943336)
XLA Ops:
  0.6 1.8 %copy.43 = bf16[1,2,128,512]{2,1,0,3:T(2,128)(2,1)} copy(bf16[1,2,128,512]{3,2,1,0:T(8,128)(2,1)} %param.23) | data formatting | bytes 524288 | tf_op args[2]
  2.5 4.8 %all-to-all-start.1 = ((bf16[1,2,128,512]{2,1,0,3:T(2,128)(2,1)}), bf16[1,2,128,512]{2,1,0,3:T(2,128)(2,1)S(1)}, u32[]{:S(2)}, u32[]{:S(2)}) async-start(bf16[1,2,128,512]{2,1,0,3:T(2,128)(2,1)} %copy.43), calls=%async_computation.1 | async-start | bytes 524288 | tf_op jit(solution)/shard_map/all_to_all | solution.py:104
  8.6 1.0 slice_bitcast_fusion.13
  9.5 1.7 %slice_bitcast_fusion.1 = (bf16[64,8,8,128]{3,1,2,0:T(8,128)(2,1)S(1)}, bf16[64,8,8,128]{3,1,2,0:T(8,128)(2,1)S(1)}) fusion(bf16[1,2,512,1024]{3,2,1,0:T(8,128)(2,1)} %param.21), kind=kLoop, calls=%fused_computation.56 | loop fusion | bytes 4194304
  11.3 4.7 %slice_bitcast_fusion.3 = (bf16[64,8,8,128]{3,1,2,0:T(8,128)(2,1)}, f32[64,8,8,128]{3,1,2,0:T(8,128)}, f32[64,8,8,128]{3,1,2,0:T(8,128)}, bf16[64,8,8,128]{3,1,2,0:T(8,128)(2,1)}) fusion(bf16[1,2,512,1024]{3,2,1,0:T(8,128)(2,1)} %param.24), kind=kLoop, calls=%fused_computation.68 | loop fusion | flops 1048576 | bytes 8388608
  16.0 0.7 pad_maximum_fusion.1
  16.8 4.8 %all-to-all-start = ((bf16[4,1,2,128,128]{4,3,2,1,0:T(8,128)(2,1)}), bf16[4,1,2,128,128]{4,3,2,1,0:T(8,128)(2,1)S(1)}, u32[]{:S(2)}, u32[]{:S(2)}) async-start(bf16[4,1,2,128,128]{4,3,2,1,0:T(8,128)(2,1)} %pad_maximum_fusion.1), calls=%async_computation | async-start | bytes 524288 | tf_op jit(solution)/shard_map/all_to_all | solution.py:101
  21.6 0.7 iota_compare_fusion
  22.5 4.3 %all-to-all-done = bf16[4,1,2,128,128]{4,3,2,1,0:T(8,128)(2,1)S(1)} async-done(((bf16[4,1,2,128,128]{4,3,2,1,0:T(8,128)(2,1)}), bf16[4,1,2,128,128]{4,3,2,1,0:T(8,128)(2,1)S(1)}, u32[]{:S(2)}, u32[]{:S(2)}) %all-to-all-start) | async-done | bytes 262176 | tf_op jit(solution)/shard_map/all_to_all | solution.py:101
  26.8 1.0 fusion.104
  27.8 0.7 maximum_bitcast_fusion.1
  28.5 5.4 %collective-permute-start.1 = (bf16[1,2,512,128]{3,2,1,0:T(8,128)(2,1)}, bf16[1,2,512,128]{3,2,1,0:T(8,128)(2,1)}, u32[]{:S(2)}, u32[]{:S(2)}) collective-permute-start(bf16[1,2,512,128]{3,2,1,0:T(8,128)(2,1)} %maximum_bitcast_fusion.1), channel_id=1, source_target_pairs={{4,0},{8,4},{12,8},{16,12},{20,16},{24,20},{28,24},{32,28},{36,32}... | collective-permute-start | bytes 786440 | tf_op jit(solution)/shard_map/ppermute | solution.py:21
  34.6 2.6 %copy.94 = bf16[64,8,8,128]{3,2,1,0:T(8,128)(2,1)} copy(bf16[64,8,8,128]{3,1,2,0:T(8,128)(2,1)} %get-tuple-element.83) | data formatting | bytes 2097152
  37.2 2.5 %copy.97 = bf16[64,8,8,128]{3,2,1,0:T(8,128)(2,1)} copy(bf16[64,8,8,128]{3,1,2,0:T(8,128)(2,1)} %get-tuple-element.86) | data formatting | bytes 2097152
  39.7 3.4 %copy.95 = f32[64,8,8,128]{3,2,1,0:T(8,128)} copy(f32[64,8,8,128]{3,1,2,0:T(8,128)} %get-tuple-element.84) | data formatting | bytes 4194304
  43.1 3.0 %copy.49 = f32[4,128,1,8,128]{1,4,3,0,2:T(8,128)} copy(f32[4,128,1,8,128]{4,3,2,1,0:T(8,128)} %bitcast.427) | data formatting | bytes 4194304 | tf_op jit(solution)/shard_map/convert_element_type | solution.py:75
  46.1 3.4 %copy.98 = f32[64,8,8,128]{3,2,1,0:T(8,128)} copy(f32[64,8,8,128]{3,1,2,0:T(8,128)} %get-tuple-element.85) | data formatting | bytes 4194304
  49.4 2.9 %copy.57 = f32[4,128,1,8,128]{1,4,3,0,2:T(8,128)} copy(f32[4,128,1,8,128]{4,3,2,1,0:T(8,128)} %bitcast.428) | data formatting | bytes 4194304 | tf_op jit(solution)/shard_map/convert_element_type | solution.py:75
  52.3 1.0 broadcast_and_fusion.1
  53.4 1.0 fusion.83
  54.4 2.1 %collective-permute-start = (bf16[1,2,512,128]{3,2,1,0:T(8,128)(2,1)S(1)}, bf16[1,2,512,128]{3,2,1,0:T(8,128)(2,1)S(1)}, u32[]{:S(2)}, u32[]{:S(2)}) collective-permute-start(bf16[1,2,512,128]{3,2,1,0:T(8,128)(2,1)S(1)} %get-tuple-element.135), channel_id=1, source_target_pairs={{0,4},{4,8},{8,12},{12,16},{16,20},{20,24},{24,28},{28,32},{32,36}... | collective-permute-start | bytes 786440 | tf_op jit(solution)/shard_map/ppermute | solution.py:19
  57.0 1.6 %fusion.6 = (f32[4,8,128]{2,1,0:T(8,128)S(1)}, f32[4,640,128,8]{2,1,3,0:T(8,128)S(1)}) fusion(pred[4,128,640]{1,2,0:T(8,128)(4,1)S(1)} %get-tuple-element.152, bf16[4,128,8,128]{3,2,1,0:T(8,128)(2,1)S(1)} %bitcast.425, bf16[4,640,1,128]{3,1,0,2:T(8,128)(2,1)S(1)} %constant_dynamic-update-slice_fusion.10), kind=kOutput, calls=%fused_computation.10 | convolution fusion | flops 678948864 | bytes 12533760 | tf_op jit(solution)/shard_map/btgjd,bkgd->bgjtk/dot_general | solution.py:65
  58.6 2.4 %fusion.15 = f32[4,8,128]{2,1,0:T(8,128)S(1)} fusion(f32[4,640,128,8]{2,1,3,0:T(8,128)S(1)} %get-tuple-element.156, f32[4,8,128]{2,1,0:T(8,128)S(1)} %get-tuple-element.155, pred[4,128,640]{1,2,0:T(8,128)(4,1)S(1)} %get-tuple-element.152), kind=kLoop, calls=%fused_computation.21 | loop fusion | flops 10481664 | bytes 10846208 | tf_op jit(solution)/shard_map/reduce_sum | solution.py:70
  61.1 3.1 %fusion.41 = f32[4,640,1,128]{3,1,0,2:T(8,128)S(1)} fusion(bf16[4,128,8,128]{3,2,1,0:T(8,128)(2,1)S(1)} %bitcast.451, f32[4,8,128]{2,1,0:T(8,128)S(1)} %fusion.15, f32[4,8,128]{2,1,0:T(8,128)S(1)} %get-tuple-element.155, f32[4,640,128,8]{2,1,3,0:T(8,128)S(1)} %get-tuple-element.156, pred[4,128,640]{1,2,0:T(8,128)(4,1)S(1)} %get-tuple-element.152), kind=kOutput, calls=%fused_computation.50 | convolution fusion | flops 684195840 | bytes 13205504 | tf_op jit(solution)/shard_map/bgjtk,btgjd->bkgd/dot_general | solution.py:88
  64.2 3.2 %fusion.29 = f32[4,128,8]{1,2,0:T(8,128)S(1)} fusion(f32[4,128,1,8,128]{1,4,3,0,2:T(8,128)S(1)} %copy-done.3, bf16[4,640,1,128]{3,1,0,2:T(8,128)(2,1)S(1)} %constant_dynamic-update-slice_fusion.15, f32[4,8,128]{2,1,0:T(8,128)S(1)} %fusion.15, f32[4,8,128]{2,1,0:T(8,128)S(1)} %get-tuple-element.155, f32[4,640,128,8]{2,1,3,0:T(8,128)S(1)} %get-tuple-element.156, ...), kind=kOutput, calls=%fused_computation.37 | convolution fusion | flops 686288896 | bytes 13615104 | tf_op jit(solution)/shard_map/bgjtk,bkgd->btgjd/dot_general | solution.py:72
  67.4 4.2 %fusion.17 = bf16[4,8,128,640]{2,3,1,0:T(8,128)(2,1)S(1)} fusion(f32[4,8,128]{2,1,0:T(8,128)S(1)} %bitcast.478, f32[4,8,128]{2,1,0:T(8,128)S(1)} %fusion.15, f32[4,8,128]{2,1,0:T(8,128)S(1)} %get-tuple-element.155, f32[4,640,128,8]{2,1,3,0:T(8,128)S(1)} %get-tuple-element.156, pred[4,128,640]{1,2,0:T(8,128)(4,1)S(1)} %get-tuple-element.152, ...), kind=kOutput, calls=%fused_computation.23 | convolution fusion | flops 692060160 | bytes 17809408 | tf_op jit(solution)/shard_map/btgjd,bkgd->bgjtk/dot_general | solution.py:76
  71.9 1.5 %convolution_bitcast_fusion = f32[4,640,1,128]{3,1,0,2:T(8,128)S(1)} fusion(bf16[4,8,128,640]{2,3,1,0:T(8,128)(2,1)S(1)} %fusion.17, bf16[4,128,8,128]{3,2,1,0:T(8,128)(2,1)S(1)} %bitcast.426), kind=kOutput, calls=%fused_computation.47 | convolution fusion | flops 671088640 | bytes 7602176 | tf_op jit(solution)/shard_map/bgjtk,btgjd->bkgd/dot_general | solution.py:85
  73.6 2.1 %collective-permute-start.2 = (bf16[1,2,512,128]{3,2,1,0:T(8,128)(2,1)S(1)}, bf16[1,2,512,128]{3,2,1,0:T(8,128)(2,1)S(1)}, u32[]{:S(2)}, u32[]{:S(2)}) collective-permute-start(bf16[1,2,512,128]{3,2,1,0:T(8,128)(2,1)S(1)} %fusion.76), channel_id=1, source_target_pairs={{0,4},{4,8},{8,12},{12,16},{16,20},{20,24},{24,28},{28,32},{32,36}... | collective-permute-start | bytes 786440 | tf_op jit(solution)/shard_map/ppermute | solution.py:19
  76.3 1.6 %fusion.9 = (f32[4,8,128]{2,1,0:T(8,128)S(1)}, f32[4,640,128,8]{2,1,3,0:T(8,128)S(1)}) fusion(pred[4,128,640]{1,2,0:T(8,128)(4,1)S(1)} %get-tuple-element.151, bf16[4,128,8,128]{3,2,1,0:T(8,128)(2,1)S(1)} %bitcast.423, bf16[4,640,1,128]{3,1,0,2:T(8,128)(2,1)S(1)} %constant_dynamic-update-slice_fusion), kind=kOutput, calls=%fused_computation.15 | convolution fusion | flops 678948864 | bytes 12533760 | tf_op jit(solution)/shard_map/btgjd,bkgd->bgjtk/dot_general | solution.py:65
  78.0 2.4 %fusion.13 = f32[4,8,128]{2,1,0:T(8,128)S(1)} fusion(f32[4,640,128,8]{2,1,3,0:T(8,128)S(1)} %get-tuple-element.158, f32[4,8,128]{2,1,0:T(8,128)S(1)} %get-tuple-element.157, pred[4,128,640]{1,2,0:T(8,128)(4,1)S(1)} %get-tuple-element.151), kind=kLoop, calls=%fused_computation.19 | loop fusion | flops 10481664 | bytes 10846208 | tf_op jit(solution)/shard_map/reduce_sum | solution.py:70
  80.4 3.1 %fusion.38 = f32[4,640,1,128]{3,1,0,2:T(8,128)S(1)} fusion(bf16[4,128,8,128]{3,2,1,0:T(8,128)(2,1)S(1)} %bitcast.449, f32[4,8,128]{2,1,0:T(8,128)S(1)} %fusion.13, f32[4,8,128]{2,1,0:T(8,128)S(1)} %get-tuple-element.157, f32[4,640,128,8]{2,1,3,0:T(8,128)S(1)} %get-tuple-element.158, pred[4,128,640]{1,2,0:T(8,128)(4,1)S(1)} %get-tuple-element.151), kind=kOutput, calls=%fused_computation.49 | convolution fusion | flops 684195840 | bytes 13205504 | tf_op jit(solution)/shard_map/bgjtk,btgjd->bkgd/dot_general | solution.py:88
  83.6 3.2 %fusion.31 = f32[4,128,8]{1,2,0:T(8,128)S(1)} fusion(f32[4,128,1,8,128]{1,4,3,0,2:T(8,128)S(1)} %copy-done.2, bf16[4,640,1,128]{3,1,0,2:T(8,128)(2,1)S(1)} %constant_dynamic-update-slice_fusion.5, f32[4,8,128]{2,1,0:T(8,128)S(1)} %fusion.13, f32[4,8,128]{2,1,0:T(8,128)S(1)} %get-tuple-element.157, f32[4,640,128,8]{2,1,3,0:T(8,128)S(1)} %get-tuple-element.158, ...), kind=kOutput, calls=%fused_computation.40 | convolution fusion | flops 686288896 | bytes 13615104 | tf_op jit(solution)/shard_map/bgjtk,bkgd->btgjd/dot_general | solution.py:72
  86.7 4.2 %fusion.16 = bf16[4,8,128,640]{2,3,1,0:T(8,128)(2,1)S(1)} fusion(f32[4,8,128]{2,1,0:T(8,128)S(1)} %bitcast.479, f32[4,8,128]{2,1,0:T(8,128)S(1)} %fusion.13, f32[4,8,128]{2,1,0:T(8,128)S(1)} %get-tuple-element.157, f32[4,640,128,8]{2,1,3,0:T(8,128)S(1)} %get-tuple-element.158, pred[4,128,640]{1,2,0:T(8,128)(4,1)S(1)} %get-tuple-element.151, ...), kind=kOutput, calls=%fused_computation.22 | convolution fusion | flops 692060160 | bytes 17809408 | tf_op jit(solution)/shard_map/btgjd,bkgd->bgjtk/dot_general | solution.py:76
  91.2 1.5 %convolution_bitcast_fusion.1 = f32[4,640,1,128]{3,1,0,2:T(8,128)S(1)} fusion(bf16[4,8,128,640]{2,3,1,0:T(8,128)(2,1)S(1)} %fusion.16, bf16[4,128,8,128]{3,2,1,0:T(8,128)(2,1)S(1)} %bitcast.424), kind=kOutput, calls=%fused_computation.48 | convolution fusion | flops 671088640 | bytes 7602176 | tf_op jit(solution)/shard_map/bgjtk,btgjd->bkgd/dot_general | solution.py:85
  93.0 5.8 %collective-permute-start.3 = (bf16[1,2,512,128]{3,2,1,0:T(8,128)(2,1)S(1)}, bf16[1,2,512,128]{3,2,1,0:T(8,128)(2,1)S(1)}, u32[]{:S(2)}, u32[]{:S(2)}) collective-permute-start(bf16[1,2,512,128]{3,2,1,0:T(8,128)(2,1)S(1)} %maximum_bitcast_fusion.2), channel_id=1, source_target_pairs={{4,0},{8,4},{12,8},{16,12},{20,16},{24,20},{28,24},{32,28},{36,32}... | collective-permute-start | bytes 786440 | tf_op jit(solution)/shard_map/ppermute | solution.py:21
  98.7 3.9 %collective-permute-done.3 = bf16[1,2,512,128]{3,2,1,0:T(8,128)(2,1)S(1)} collective-permute-done((bf16[1,2,512,128]{3,2,1,0:T(8,128)(2,1)S(1)}, bf16[1,2,512,128]{3,2,1,0:T(8,128)(2,1)S(1)}, u32[]{:S(2)}, u32[]{:S(2)}) %collective-permute-start.3) | collective-permute-done | bytes 262176 | tf_op jit(solution)/shard_map/ppermute | solution.py:21
  102.9 1.0 copy.67
  103.9 4.8 %all-to-all-start.3 = ((bf16[1,2,512,128]{3,1,0,2:T(2,128)(2,1)}), bf16[1,2,512,128]{3,1,0,2:T(2,128)(2,1)S(1)}, u32[]{:S(2)}, u32[]{:S(2)}) async-start(bf16[1,2,512,128]{3,1,0,2:T(2,128)(2,1)} %copy.67), calls=%async_computation.3 | async-start | bytes 524288 | tf_op jit(solution)/shard_map/all_to_all | solution.py:168
  108.7 4.5 %fusion.45 = bf16[4,128,1,8,128]{1,4,3,0,2:T(8,128)(2,1)} fusion(bf16[4,8,128,640]{2,3,1,0:T(8,128)(2,1)} %copy-done, bf16[4,640,1,128]{3,1,0,2:T(8,128)(2,1)S(1)} %constant_dynamic-update-slice_fusion.10), kind=kOutput, calls=%fused_computation.52 | convolution fusion | flops 671612928 | bytes 6946816 | tf_op jit(solution)/shard_map/bgjtk,bkgd->btgjd/dot_general | solution.py:82
  113.2 1.7 %copy.60 = bf16[4,128,1,8,128]{4,3,1,0,2:T(8,128)(2,1)S(1)} copy(bf16[4,128,1,8,128]{1,4,3,0,2:T(8,128)(2,1)} %fusion.45) | data formatting | bytes 2097152 | tf_op jit(solution)/shard_map/convert_element_type | solution.py:84
  115.4 1.0 copy.65
  116.4 4.8 %all-to-all-start.2 = ((bf16[1,2,512,128]{3,1,0,2:T(2,128)(2,1)}), bf16[1,2,512,128]{3,1,0,2:T(2,128)(2,1)S(1)}, u32[]{:S(2)}, u32[]{:S(2)}) async-start(bf16[1,2,512,128]{3,1,0,2:T(2,128)(2,1)} %copy.65), calls=%async_computation.2 | async-start | bytes 524288 | tf_op jit(solution)/shard_map/all_to_all | solution.py:167
  121.2 4.5 %fusion.44 = bf16[4,128,1,8,128]{1,4,3,0,2:T(8,128)(2,1)} fusion(bf16[4,8,128,640]{2,3,1,0:T(8,128)(2,1)} %copy-done.1, bf16[4,640,1,128]{3,1,0,2:T(8,128)(2,1)S(1)} %constant_dynamic-update-slice_fusion), kind=kOutput, calls=%fused_computation.51 | convolution fusion | flops 671612928 | bytes 6946816 | tf_op jit(solution)/shard_map/bgjtk,bkgd->btgjd/dot_general | solution.py:82
  125.7 1.7 %copy.52 = bf16[4,128,1,8,128]{4,3,1,0,2:T(8,128)(2,1)S(1)} copy(bf16[4,128,1,8,128]{1,4,3,0,2:T(8,128)(2,1)} %fusion.44) | data formatting | bytes 2097152 | tf_op jit(solution)/shard_map/convert_element_type | solution.py:84
  127.4 1.3 stack_reshape.6
  128.6 2.7 %maximum_bitcast_fusion = bf16[1,2,512,1024]{3,2,1,0:T(8,128)(2,1)} fusion(bf16[1,512,1024]{2,1,0:T(8,128)(2,1)S(1)} %stack_reshape.7, bf16[1,512,1024]{2,1,0:T(8,128)(2,1)} %stack_reshape.6), kind=kLoop, calls=%fused_computation.34 | loop fusion | flops 1048576 | bytes 4194304 | tf_op jit(solution)/shard_map/broadcast_in_dim | solution.py:163
  131.6 0.8 all_to_all.54
  132.6 0.8 all_to_all.50
  (97 shorter events, 5.0 us)
Async XLA Ops:
  2.5 14.3 %all-to-all-start.1 = ((bf16[1,2,128,512]{2,1,0,3:T(2,128)(2,1)}), bf16[1,2,128,512]{2,1,0,3:T(2,128)(2,1)S(1)}, u32[]{:S(2)}, u32[]{:S(2)}) async-start(bf16[1,2,128,512]{2,1,0,3:T(2,128)(2,1)} %copy.43), calls=%async_computation.1 | async-start | bytes 524288 | tf_op jit(solution)/shard_map/all_to_all | solution.py:104
  16.8 10.0 %all-to-all-start = ((bf16[4,1,2,128,128]{4,3,2,1,0:T(8,128)(2,1)}), bf16[4,1,2,128,128]{4,3,2,1,0:T(8,128)(2,1)S(1)}, u32[]{:S(2)}, u32[]{:S(2)}) async-start(bf16[4,1,2,128,128]{4,3,2,1,0:T(8,128)(2,1)} %pad_maximum_fusion.1), calls=%async_computation | async-start | bytes 524288 | tf_op jit(solution)/shard_map/all_to_all | solution.py:101
  28.5 24.8 %collective-permute-start.1 = (bf16[1,2,512,128]{3,2,1,0:T(8,128)(2,1)}, bf16[1,2,512,128]{3,2,1,0:T(8,128)(2,1)}, u32[]{:S(2)}, u32[]{:S(2)}) collective-permute-start(bf16[1,2,512,128]{3,2,1,0:T(8,128)(2,1)} %maximum_bitcast_fusion.1), channel_id=1, source_target_pairs={{4,0},{8,4},{12,8},{16,12},{20,16},{24,20},{28,24},{32,28},{36,32}... | collective-permute-start | bytes 786440 | tf_op jit(solution)/shard_map/ppermute | solution.py:21
  34.5 17.8 %copy-start.13 = (pred[128,640]{0,1:T(8,128)(4,1)S(1)}, pred[128,640]{0,1:T(8,128)(4,1)}, u32[]{:S(2)}) copy-start(pred[128,640]{0,1:T(8,128)(4,1)} %iota_compare_fusion) | copy-start | bytes 245764
  34.6 18.8 %copy-start.11 = (bf16[1,512,128]{2,1,0:T(8,128)(2,1)S(1)}, bf16[1,512,128]{2,1,0:T(8,128)(2,1)}, u32[]{:S(2)}) copy-start(bf16[1,512,128]{2,1,0:T(8,128)(2,1)} %get-tuple-element.114) | copy-start | bytes 393220
  34.6 18.8 %copy-start.12 = (bf16[1,512,128]{2,1,0:T(8,128)(2,1)S(1)}, bf16[1,512,128]{2,1,0:T(8,128)(2,1)}, u32[]{:S(2)}) copy-start(bf16[1,512,128]{2,1,0:T(8,128)(2,1)} %get-tuple-element.163) | copy-start | bytes 393220
  37.2 19.4 %copy-start.6 = (bf16[512,128]{1,0:T(8,128)(2,1)S(1)}, bf16[512,128]{1,0:T(8,128)(2,1)}, u32[]{:S(2)}) copy-start(bf16[512,128]{1,0:T(8,128)(2,1)} %get-tuple-element.117) | copy-start | bytes 393220
  39.7 17.1 %copy-start.10 = (bf16[1,1,512,128]{3,2,1,0:T(8,128)(2,1)S(1)}, bf16[1,1,512,128]{3,2,1,0:T(8,128)(2,1)}, u32[]{:S(2)}) copy-start(bf16[1,1,512,128]{3,2,1,0:T(8,128)(2,1)} %get-tuple-element.159) | copy-start | bytes 393220
  43.1 13.8 %copy-start.9 = (bf16[1,1,512,128]{3,2,1,0:T(8,128)(2,1)S(1)}, bf16[1,1,512,128]{3,2,1,0:T(8,128)(2,1)}, u32[]{:S(2)}) copy-start(bf16[1,1,512,128]{3,2,1,0:T(8,128)(2,1)} %get-tuple-element.118) | copy-start | bytes 393220
  54.4 21.4 %collective-permute-start = (bf16[1,2,512,128]{3,2,1,0:T(8,128)(2,1)S(1)}, bf16[1,2,512,128]{3,2,1,0:T(8,128)(2,1)S(1)}, u32[]{:S(2)}, u32[]{:S(2)}) collective-permute-start(bf16[1,2,512,128]{3,2,1,0:T(8,128)(2,1)S(1)} %get-tuple-element.135), channel_id=1, source_target_pairs={{0,4},{4,8},{8,12},{12,16},{16,20},{20,24},{24,28},{28,32},{32,36}... | collective-permute-start | bytes 786440 | tf_op jit(solution)/shard_map/ppermute | solution.py:19
  56.9 4.1 %copy-start.5 = (bf16[64,8,8,128]{3,2,1,0:T(8,128)(2,1)S(1)}, bf16[64,8,8,128]{3,2,1,0:T(8,128)(2,1)}, u32[]{:S(2)}) copy-start(bf16[64,8,8,128]{3,2,1,0:T(8,128)(2,1)} %copy.97) | copy-start | bytes 3145732
  61.1 3.1 %copy-start.3 = (f32[4,128,1,8,128]{1,4,3,0,2:T(8,128)S(1)}, f32[4,128,1,8,128]{1,4,3,0,2:T(8,128)}, u32[]{:S(2)}) copy-start(f32[4,128,1,8,128]{1,4,3,0,2:T(8,128)} %copy.57) | copy-start | bytes 6291460
  71.6 4.4 %copy-start = (bf16[4,8,128,640]{2,3,1,0:T(8,128)(2,1)}, bf16[4,8,128,640]{2,3,1,0:T(8,128)(2,1)S(1)}, u32[]{:S(2)}) copy-start(bf16[4,8,128,640]{2,3,1,0:T(8,128)(2,1)S(1)} %fusion.17) | copy-start | bytes 15728644
  71.6 4.5 %copy-start.8 = (bf16[1,1,512,128]{3,2,1,0:T(8,128)(2,1)S(1)}, bf16[1,1,512,128]{3,2,1,0:T(8,128)(2,1)}, u32[]{:S(2)}) copy-start(bf16[1,1,512,128]{3,2,1,0:T(8,128)(2,1)} %get-tuple-element.164) | copy-start | bytes 393220
  71.7 4.5 %copy-start.7 = (bf16[1,1,512,128]{3,2,1,0:T(8,128)(2,1)S(1)}, bf16[1,1,512,128]{3,2,1,0:T(8,128)(2,1)}, u32[]{:S(2)}) copy-start(bf16[1,1,512,128]{3,2,1,0:T(8,128)(2,1)} %get-tuple-element.113) | copy-start | bytes 393220
  73.6 25.1 %collective-permute-start.2 = (bf16[1,2,512,128]{3,2,1,0:T(8,128)(2,1)S(1)}, bf16[1,2,512,128]{3,2,1,0:T(8,128)(2,1)S(1)}, u32[]{:S(2)}, u32[]{:S(2)}) collective-permute-start(bf16[1,2,512,128]{3,2,1,0:T(8,128)(2,1)S(1)} %fusion.76), channel_id=1, source_target_pairs={{0,4},{4,8},{8,12},{12,16},{16,20},{20,24},{24,28},{28,32},{32,36}... | collective-permute-start | bytes 786440 | tf_op jit(solution)/shard_map/ppermute | solution.py:19
  76.3 4.1 %copy-start.4 = (bf16[64,8,8,128]{3,2,1,0:T(8,128)(2,1)S(1)}, bf16[64,8,8,128]{3,2,1,0:T(8,128)(2,1)}, u32[]{:S(2)}) copy-start(bf16[64,8,8,128]{3,2,1,0:T(8,128)(2,1)} %copy.94) | copy-start | bytes 3145732
  80.4 3.1 %copy-start.2 = (f32[4,128,1,8,128]{1,4,3,0,2:T(8,128)S(1)}, f32[4,128,1,8,128]{1,4,3,0,2:T(8,128)}, u32[]{:S(2)}) copy-start(f32[4,128,1,8,128]{1,4,3,0,2:T(8,128)} %copy.49) | copy-start | bytes 6291460
  91.0 11.8 %copy-start.1 = (bf16[4,8,128,640]{2,3,1,0:T(8,128)(2,1)}, bf16[4,8,128,640]{2,3,1,0:T(8,128)(2,1)S(1)}, u32[]{:S(2)}) copy-start(bf16[4,8,128,640]{2,3,1,0:T(8,128)(2,1)S(1)} %fusion.16) | copy-start | bytes 15728644
  93.0 9.6 %collective-permute-start.3 = (bf16[1,2,512,128]{3,2,1,0:T(8,128)(2,1)S(1)}, bf16[1,2,512,128]{3,2,1,0:T(8,128)(2,1)S(1)}, u32[]{:S(2)}, u32[]{:S(2)}) collective-permute-start(bf16[1,2,512,128]{3,2,1,0:T(8,128)(2,1)S(1)} %maximum_bitcast_fusion.2), channel_id=1, source_target_pairs={{4,0},{8,4},{12,8},{16,12},{20,16},{24,20},{28,24},{32,28},{36,32}... | collective-permute-start | bytes 786440 | tf_op jit(solution)/shard_map/ppermute | solution.py:21
  103.9 12.5 %all-to-all-start.3 = ((bf16[1,2,512,128]{3,1,0,2:T(2,128)(2,1)}), bf16[1,2,512,128]{3,1,0,2:T(2,128)(2,1)S(1)}, u32[]{:S(2)}, u32[]{:S(2)}) async-start(bf16[1,2,512,128]{3,1,0,2:T(2,128)(2,1)} %copy.67), calls=%async_computation.3 | async-start | bytes 524288 | tf_op jit(solution)/shard_map/all_to_all | solution.py:168
  116.4 16.0 %all-to-all-start.2 = ((bf16[1,2,512,128]{3,1,0,2:T(2,128)(2,1)}), bf16[1,2,512,128]{3,1,0,2:T(2,128)(2,1)S(1)}, u32[]{:S(2)}, u32[]{:S(2)}) async-start(bf16[1,2,512,128]{3,1,0,2:T(2,128)(2,1)} %copy.65), calls=%async_computation.2 | async-start | bytes 524288 | tf_op jit(solution)/shard_map/all_to_all | solution.py:167
